TPU v7x, 32 devices: a whole 2x2x4 slice. The times are simulated.
32 devices in a mesh: replica: 2 (over y), shard: 2 (over x), tensor: 8 (over z, core).
Axes of the slice: x: 2, y: 2, z: 4, core: 2. Of those that a mesh axis runs over, the one named last changes fastest.
Arguments:
- layer_input: bfloat16 [32768, 1024], P(('replica', 'shard', 'tensor')), may hold values from -6 to 6
- segment_ids: int32 [32, 1024], P(('replica', 'shard')), may hold values from 0 to 3, as said below
- qkv_weight: bfloat16 [3, 1024, 1024], P(None, 'shard', 'tensor'), may hold values from -0.1875 to 0.1875
- qkv_bias: float32 [2, 1024], P(None, 'tensor'), may hold values from -1.2 to 1.2
- out_weight: bfloat16 [1024, 1024], P('tensor', 'shard'), may hold values from -1.5 to 1.5
- out_bias: float32 [1024], replicated, may hold values from -3 to 3
- norm1_gain: float32 [1024], replicated, may hold values from 0.5 to 1.5
- norm1_bias: float32 [1024], replicated, may hold values from -3 to 3
- up_weight: bfloat16 [1024, 4096], P('shard', 'tensor'), may hold values from -0.1875 to 0.1875
- up_bias: float32 [4096], P('tensor'), may hold values from -3 to 3
- down_weight: bfloat16 [4096, 1024], P('tensor', 'shard'), may hold values from -0.09375 to 0.09375
- down_bias: float32 [1024], replicated, may hold values from -3 to 3
- norm2_gain: float32 [1024], replicated, may hold values from 0.5 to 1.5
- norm2_bias: float32 [1024], replicated, may hold values from -3 to 3
- output_grad: bfloat16 [32768, 1024], P(('replica', 'shard', 'tensor')), may hold values from -6 to 6
Outputs:
- activations: bfloat16 [32768, 1024], P(('replica', 'shard', 'tensor'))
- input_grad: float32 [32768, 1024], P(('replica', 'shard', 'tensor'))
- qkv_weight_grad: float32 [3, 1024, 1024], P(None, 'shard', 'tensor')
- qkv_bias_grad: float32 [2, 1024], P(None, 'tensor')
- out_weight_grad: float32 [1024, 1024], P('tensor', 'shard')
- out_bias_grad: float32 [1024], replicated
- norm1_gain_grad: float32 [1024], replicated
- norm1_bias_grad: float32 [1024], replicated
- up_weight_grad: float32 [1024, 4096], P('shard', 'tensor')
- up_bias_grad: float32 [4096], P('tensor')
- down_weight_grad: float32 [4096, 1024], P('tensor', 'shard')
- down_bias_grad: float32 [1024], replicated
- norm2_gain_grad: float32 [1024], replicated
- norm2_bias_grad: float32 [1024], replicated
Inputs may be any that keep to these rules, and one draw needn't show every extreme that they name: `segment_ids`: within each sequence the ids never fall and every id from 0 to 3 occurs; each document holds 128 to 512 tokens, and one in each sequence holds exactly 512.
All inputs are finite; a program needn't handle non-finite values.
Results may differ from a plain program's by a relative error of at most 0.02.
Values may be sent and summed in bfloat16 or wider, within the bound.
No kernel may reach another device: no remote copies, remote signals or barrier semaphores. Data moves between devices by JAX's collectives and lax.ppermute only.
A program may use at most 256 MiB of HBM per device.

v0:
```python
import math
import jax
import jax.numpy as jnp
from jax import lax
from jax.sharding import PartitionSpec as P

HEAD_DIM = 64
LEN = 1024
EPSILON = 1e-05
NEG_FILL = -1e30
CONTRACT_ROWS = (((0,), (0,)), ((), ()))
CONTRACT_COLS = (((1,), (1,)), ((), ()))


def layer_weights(qkv_weight, out_weight, up_weight, down_weight):
    return (
        lax.all_gather(qkv_weight, "shard", axis=1, tiled=True),
        lax.all_gather(out_weight, "shard", axis=1, tiled=True),
        lax.all_gather(up_weight, "shard", axis=0, tiled=True),
        lax.all_gather(down_weight, "shard", axis=1, tiled=True),
    )


def input_rows(layer_input):
    return lax.all_gather(layer_input, "tensor", axis=0, tiled=True)


def middle_rows(hidden_low):
    return lax.all_gather(hidden_low, "tensor", axis=0, tiled=True)


def normalize(residual, gain_vec, shift_vec):
    center = residual - jnp.mean(residual, axis=-1, keepdims=True)
    spread = lax.rsqrt(jnp.mean(center * center, axis=-1, keepdims=True) + EPSILON)
    normed = center * spread
    return (normed * gain_vec + shift_vec, normed, spread)


def norm_back(incoming, normed, spread, gain_vec):
    scaled = incoming * gain_vec
    back_grad = spread * (
        scaled
        - jnp.mean(scaled, axis=-1, keepdims=True)
        - normed * jnp.mean(scaled * normed, axis=-1, keepdims=True)
    )
    return (back_grad, jnp.sum(incoming * normed, axis=0), jnp.sum(incoming, axis=0))


def masked_scores(queries, key_rows, segments):
    scores = jnp.einsum(
        "qhd,khd->hqk", queries, key_rows, preferred_element_type=jnp.float32
    ) * HEAD_DIM ** (-0.5)
    same_doc = segments[:, None] == segments[None, :]
    return jnp.where(same_doc[None], scores, NEG_FILL)


def attend(block_item):
    queries, key_rows, value_rows, segments = block_item
    scores = masked_scores(queries, key_rows, segments)
    row_max = jnp.max(scores, axis=-1, keepdims=True)
    raw_weights = jnp.exp(scores - row_max)
    row_total = jnp.sum(raw_weights, axis=-1, keepdims=True)
    attn_probs = raw_weights / row_total
    log_total = row_max + jnp.log(row_total)
    mixed_heads = jnp.einsum(
        "hqk,khd->qhd",
        attn_probs.astype(jnp.bfloat16),
        value_rows,
        preferred_element_type=jnp.float32,
    )
    return (mixed_heads.astype(jnp.bfloat16), log_total)


def attend_back(block_item):
    queries, key_rows, value_rows, segments, log_total, mixed_grad = block_item
    scores = masked_scores(queries, key_rows, segments)
    attn_probs = jnp.exp(scores - log_total)
    prob_grad = jnp.einsum(
        "qhd,khd->hqk", mixed_grad, value_rows, preferred_element_type=jnp.float32
    )
    value_grad = jnp.einsum(
        "hqk,qhd->khd",
        attn_probs.astype(jnp.bfloat16),
        mixed_grad,
        preferred_element_type=jnp.float32,
    )
    inner_sum = jnp.sum(attn_probs * prob_grad, axis=-1, keepdims=True)
    score_low = (attn_probs * (prob_grad - inner_sum)).astype(jnp.bfloat16)
    query_grad = jnp.einsum(
        "hqk,khd->qhd", score_low, key_rows, preferred_element_type=jnp.float32
    ) * HEAD_DIM ** (-0.5)
    key_grad = jnp.einsum(
        "hqk,qhd->khd", score_low, queries, preferred_element_type=jnp.float32
    ) * HEAD_DIM ** (-0.5)
    return (query_grad, key_grad, value_grad)


def body(
    layer_input,
    segment_ids,
    qkv_weight,
    qkv_bias,
    out_weight,
    out_bias,
    norm1_gain,
    norm1_bias,
    up_weight,
    up_bias,
    down_weight,
    down_bias,
    norm2_gain,
    norm2_bias,
    output_grad,
):
    rows_input = input_rows(layer_input)
    group_rows = rows_input.shape[0]
    seq_count = group_rows // LEN
    w_qkv, w_out, w_up, w_down = layer_weights(qkv_weight, out_weight, up_weight, down_weight)
    width = w_qkv.shape[2]
    heads_here = width // HEAD_DIM
    hidden_here = w_up.shape[1]

    def split_heads(rows_array):
        return rows_array.reshape(seq_count, LEN, heads_here, HEAD_DIM)

    projected = jnp.einsum("td,jdc->jtc", rows_input, w_qkv, preferred_element_type=jnp.float32)
    queries = (projected[0] + qkv_bias[0]).astype(jnp.bfloat16)
    key_rows = projected[1].astype(jnp.bfloat16)
    value_rows = (projected[2] + qkv_bias[1]).astype(jnp.bfloat16)
    mixed, log_total = lax.map(
        attend, (split_heads(queries), split_heads(key_rows), split_heads(value_rows), segment_ids)
    )
    mixed_rows = mixed.reshape(group_rows, width)
    row_block = mixed_rows
    attn_local = lax.psum_scatter(
        jnp.dot(row_block, w_out, preferred_element_type=jnp.float32).astype(jnp.bfloat16),
        "tensor",
        scatter_dimension=0,
        tiled=True,
    ).astype(jnp.float32)
    residual_one = layer_input.astype(jnp.float32) + attn_local + out_bias
    hidden_one, normed_one, spread_one = normalize(residual_one, norm1_gain, norm1_bias)
    hidden_low = hidden_one.astype(jnp.bfloat16)
    rows_middle = middle_rows(hidden_low)
    pre_act = jnp.dot(rows_middle, w_up, preferred_element_type=jnp.float32) + up_bias
    activ = jax.nn.gelu(pre_act, approximate=False).astype(jnp.bfloat16)
    row_block = activ
    mlp_local = lax.psum_scatter(
        jnp.dot(row_block, w_down, preferred_element_type=jnp.float32).astype(jnp.bfloat16),
        "tensor",
        scatter_dimension=0,
        tiled=True,
    ).astype(jnp.float32)
    residual_two = hidden_one + mlp_local + down_bias
    final_out, normed_two, spread_two = normalize(residual_two, norm2_gain, norm2_bias)
    resid_two_grad, gain_two_grad, shift_two_grad = norm_back(
        output_grad.astype(jnp.float32), normed_two, spread_two, norm2_gain
    )
    down_bias_part = jnp.sum(resid_two_grad, axis=0)
    branch_grad = resid_two_grad.astype(jnp.bfloat16)
    rows_branch = lax.all_gather(branch_grad, "tensor", axis=0, tiled=True)
    w_qkv, w_out, w_up, w_down = layer_weights(qkv_weight, out_weight, up_weight, down_weight)
    down_grad = lax.dot_general(
        activ, rows_branch, CONTRACT_ROWS, preferred_element_type=jnp.float32
    )
    activ_grad = lax.dot_general(
        rows_branch, w_down, CONTRACT_COLS, preferred_element_type=jnp.float32
    )
    normal_cdf = 0.5 * (1.0 + lax.erf(pre_act * (1.0 / math.sqrt(2.0))))
    normal_pdf = jnp.exp(-0.5 * pre_act * pre_act) * (1.0 / math.sqrt(2.0 * math.pi))
    pre_grad = activ_grad * (normal_cdf + pre_act * normal_pdf)
    up_bias_part = jnp.sum(pre_grad, axis=0)
    pre_low = pre_grad.astype(jnp.bfloat16)
    up_grad = lax.dot_general(
        rows_middle, pre_low, CONTRACT_ROWS, preferred_element_type=jnp.float32
    )
    row_block = pre_low
    back_middle = lax.psum_scatter(
        lax.dot_general(row_block, w_up, CONTRACT_COLS, preferred_element_type=jnp.float32),
        "tensor",
        scatter_dimension=0,
        tiled=True,
    )
    resid_one_grad, gain_one_grad, shift_one_grad = norm_back(
        resid_two_grad + back_middle, normed_one, spread_one, norm1_gain
    )
    out_bias_part = jnp.sum(resid_one_grad, axis=0)
    attn_grad = resid_one_grad.astype(jnp.bfloat16)
    rows_attn = lax.all_gather(attn_grad, "tensor", axis=0, tiled=True)
    out_grad_part = lax.dot_general(
        mixed_rows, rows_attn, CONTRACT_ROWS, preferred_element_type=jnp.float32
    )
    mixed_grad = lax.dot_general(
        rows_attn, w_out, CONTRACT_COLS, preferred_element_type=jnp.float32
    ).astype(jnp.bfloat16)
    query_grad, key_grad, value_grad = lax.map(
        attend_back,
        (
            split_heads(queries),
            split_heads(key_rows),
            split_heads(value_rows),
            segment_ids,
            log_total,
            split_heads(mixed_grad),
        ),
    )
    query_grad = query_grad.reshape(group_rows, width)
    key_grad = key_grad.reshape(group_rows, width)
    value_grad = value_grad.reshape(group_rows, width)
    bias_part = jnp.stack([jnp.sum(query_grad, axis=0), jnp.sum(value_grad, axis=0)])
    proj_low = jnp.stack([query_grad, key_grad, value_grad]).astype(jnp.bfloat16)
    qkv_grad = jnp.einsum("td,jtc->jdc", rows_input, proj_low, preferred_element_type=jnp.float32)
    row_block = proj_low
    back_input = lax.psum_scatter(
        jnp.einsum("jtc,jdc->td", row_block, w_qkv, preferred_element_type=jnp.float32).astype(
            jnp.bfloat16
        ),
        "tensor",
        scatter_dimension=0,
        tiled=True,
    ).astype(jnp.float32)
    input_grad = resid_one_grad + back_input
    qkv_owned, out_owned, up_owned, down_owned = (
        lax.psum_scatter(
            qkv_grad.astype(jnp.bfloat16), "shard", scatter_dimension=1, tiled=True
        ).astype(jnp.float32),
        lax.psum_scatter(
            out_grad_part.astype(jnp.bfloat16), "shard", scatter_dimension=1, tiled=True
        ).astype(jnp.float32),
        lax.psum_scatter(
            up_grad.astype(jnp.bfloat16), "shard", scatter_dimension=0, tiled=True
        ).astype(jnp.float32),
        lax.psum_scatter(
            down_grad.astype(jnp.bfloat16), "shard", scatter_dimension=1, tiled=True
        ).astype(jnp.float32),
    )
    qkv_owned, out_owned, up_owned, down_owned = (
        lax.psum(qkv_owned.astype(jnp.bfloat16), "replica").astype(jnp.float32),
        lax.psum(out_owned.astype(jnp.bfloat16), "replica").astype(jnp.float32),
        lax.psum(up_owned.astype(jnp.bfloat16), "replica").astype(jnp.float32),
        lax.psum(down_owned.astype(jnp.bfloat16), "replica").astype(jnp.float32),
    )
    tensor_index = lax.axis_index("tensor")
    tensor_count = lax.axis_size("tensor")
    bias_full = lax.dynamic_update_slice(
        jnp.zeros((2, width * tensor_count), jnp.float32),
        bias_part,
        (jnp.int32(0), tensor_index * width),
    )
    up_full = lax.dynamic_update_slice_in_dim(
        jnp.zeros((hidden_here * tensor_count,), jnp.float32),
        up_bias_part,
        tensor_index * hidden_here,
        0,
    )
    summed = lax.psum(
        (
            bias_full,
            up_full,
            out_bias_part,
            gain_one_grad,
            shift_one_grad,
            down_bias_part,
            gain_two_grad,
            shift_two_grad,
        ),
        ("replica", "shard", "tensor"),
    )
    qkv_bias_grad = lax.dynamic_slice_in_dim(summed[0], tensor_index * width, width, 1)
    up_bias_grad = lax.dynamic_slice_in_dim(summed[1], tensor_index * hidden_here, hidden_here, 0)
    return (
        final_out.astype(jnp.bfloat16),
        input_grad,
        qkv_owned,
        qkv_bias_grad,
        out_owned,
        summed[2],
        summed[3],
        summed[4],
        up_owned,
        up_bias_grad,
        down_owned,
        summed[5],
        summed[6],
        summed[7],
    )


def solution(mesh):
    placed = (
        P(("replica", "shard", "tensor"), None),
        P(("replica", "shard"), None),
        P(None, "shard", "tensor"),
        P(None, "tensor"),
        P("tensor", "shard"),
        P(),
        P(),
        P(),
        P("shard", "tensor"),
        P("tensor"),
        P("tensor", "shard"),
        P(),
        P(),
        P(),
        P(("replica", "shard", "tensor"), None),
    )
    return jax.shard_map(
        body,
        mesh=mesh,
        in_specs=placed,
        out_specs=(
            P(("replica", "shard", "tensor"), None),
            P(("replica", "shard", "tensor"), None),
            P(None, "shard", "tensor"),
            P(None, "tensor"),
            P("tensor", "shard"),
            P(),
            P(),
            P(),
            P("shard", "tensor"),
            P("tensor"),
            P("tensor", "shard"),
            P(),
            P(),
            P(),
        ),
        check_vma=False,
    )
```

profile of v0, /device:TPU:0, one launch (start us, length us, event | category | flops | bytes accessed | tf_op | source)
XLA Modules:
  0.0 2068.1 jit_solution(11723061719145368283)
XLA Ops:
  10.9 7.4 all_gather.30
  18.3 10.9 all_gather.28
  29.3 135.0 %all-gather.7.cloned.1.call-done = bf16[8192,1024]{1,0:T(8,128)(2,1)} async-done(((bf16[1024,1024]{1,0:T(8,128)(2,1)}), bf16[8192,1024]{1,0:T(8,128)(2,1)}) %all-gather.7.cloned.1.call-update) | async-done | bytes 16777232 | tf_op jit(solution)/shard_map/all_gather | solution.py:25
  164.3 13.2 fusion.73
  179.9 4.4 fusion.104
  184.3 3.6 copy.81
  187.9 3.6 copy.80
  194.1 7.1 fusion.83
  201.2 90.2 %while.26 = (s32[]{:T(128)}, bf16[8,1024,2,64]{1,3,2,0:T(8,128)(2,1)}, f32[8,2,1024,1]{2,1,3,0:T(2,128)}, bf16[8,1024,2,64]{1,3,2,0:T(8,128)(2,1)}, s32[8,1024]{...) while((s32[]{:T(128)}, ...), condition=%wide.region_3.4_spmd, body=%wide.region_0.3_spmd.sunk | while | flops 563214336 | bytes 30488676 | solution.py:130
  207.4 4.4 fusion.151
  218.7 4.4 fusion.151
  230.0 4.4 fusion.151
  241.3 4.4 fusion.151
  252.6 4.4 fusion.151
  263.8 4.4 fusion.151
  275.1 4.4 fusion.151
  286.4 4.4 fusion.151
  291.4 3.5 copy.53
  296.4 8.3 convolution_convert_fusion
  305.3 165.9 %reduce-scatter.9.cloned.1.call-done = bf16[1024,1024]{1,0:T(8,128)(2,1)} async-done(((bf16[8192,1024]{1,0:T(8,128)(2,1)}), bf16[1024,1024]{1,0:T(8,128)(2,1)}) %reduce-scatter.9.cloned.1.call-update) | async-done | bytes 2097168 | tf_op jit(solution)/shard_map/reduce_scatter | solution.py:135
  478.0 148.9 %all-gather.9.cloned.1.call-done = bf16[8192,1024]{1,0:T(8,128)(2,1)} async-done(((bf16[1024,1024]{1,0:T(8,128)(2,1)}), bf16[8192,1024]{1,0:T(8,128)(2,1)}) %all-gather.9.cloned.1.call-update) | async-done | bytes 16777232 | tf_op jit(solution)/shard_map/all_gather | solution.py:29
  626.8 47.4 %fusion.56 = (bf16[8192,512]{1,0:T(8,128)(2,1)}, f32[8192,512]{1,0:T(8,128)}) fusion(f32[512]{0:T(512)S(1)} %copy-done.31, bf16[8192,1024]{1,0:T(8,128)(2,1)} %all-gather.9.cloned.1.call-done, bf16[1024,512]{1,0:T(8,128)(2,1)} %all-gather.11.cloned.1.call-done), kind=kOutput, calls=%fused_computation.68 | convolution fusion | flops 8866758656 | bytes 42993664 | tf_op jit(solution)/shard_map/dot_general | solution.py:145
  674.2 14.8 convolution_convert_fusion.1
  689.0 166.3 %reduce-scatter.11.cloned.1.call-done = bf16[1024,1024]{1,0:T(8,128)(2,1)} async-done(((bf16[8192,1024]{1,0:T(8,128)(2,1)}), bf16[1024,1024]{1,0:T(8,128)(2,1)}) %reduce-scatter.11.cloned.1.call-update) | async-done | bytes 2097168 | tf_op jit(solution)/shard_map/reduce_scatter | solution.py:148
  855.3 4.2 fusion.103
  864.0 3.6 fusion.100
  871.4 149.7 %all-gather.15.cloned.1.call-done = bf16[8192,1024]{1,0:T(8,128)(2,1)} async-done(((bf16[1024,1024]{1,0:T(8,128)(2,1)}), bf16[8192,1024]{1,0:T(8,128)(2,1)}) %all-gather.15.cloned.1.call-update) | async-done | bytes 16777232 | tf_op jit(solution)/shard_map/all_gather | solution.py:161
  1021.1 22.2 %fusion.107 = (f32[512]{0:T(512)}, bf16[8192,512]{1,0:T(8,128)(2,1)}) fusion(f32[8192,512]{1,0:T(8,128)} %get-tuple-element.248, f32[512]{0:T(512)S(1)} %copy-done.31, bf16[8192,1024]{1,0:T(8,128)(2,1)} %all-gather.15.cloned.1.call-done, bf16[512,1024]{1,0:T(8,128)(2,1)S(1)} %copy-done.30), kind=kOutput, calls=%fused_computation.157 | convolution fusion | flops 8640266240 | bytes 42995712 | tf_op jit(solution)/shard_map/dot_general | solution.py:166
  1043.3 18.7 fusion.87
  1062.1 323.6 %reduce-scatter.13.cloned.1.call-done = f32[1024,1024]{1,0:T(8,128)} async-done(((f32[8192,1024]{1,0:T(8,128)}), f32[1024,1024]{1,0:T(8,128)}) %reduce-scatter.13.cloned.1.call-update) | async-done | bytes 4194320 | tf_op jit(solution)/shard_map/reduce_scatter | solution.py:178
  1385.7 6.6 multiply_reduce_fusion.1
  1398.6 15.9 fusion.91
  1414.7 16.2 convolution_convert_fusion.3
  1430.9 117.4 %all-gather.17.cloned.1.call-done = bf16[8192,1024]{1,0:T(8,128)(2,1)} async-done(((bf16[1024,1024]{1,0:T(8,128)(2,1)}), bf16[8192,1024]{1,0:T(8,128)(2,1)}) %all-gather.17.cloned.1.call-update) | async-done | bytes 16777232 | tf_op jit(solution)/shard_map/all_gather | solution.py:189
  1548.3 8.3 convolution_convert_fusion.2
  1556.7 3.3 reshape.197
  1560.0 9.1 copy.56
  1569.1 160.9 %while.27 = (s32[]{:T(128)}, f32[8,1024,2,64]{1,3,2,0:T(8,128)}, bf16[8,1024,2,64]{1,3,2,0:T(8,128)(2,1)}, f32[8,1024,2,64]{1,3,2,0:T(8,128)}, bf16[8,1024,2,64]...) while((s32[]{:T(128)}, f32[8,1024,2,64]{1,3,2,0:T(8,128)}, ...), condition=%wide.region_17.18_spmd, body=%wide.region_15.17_spmd.sunk | while | flops 1374943232 | bytes 70591616 | solution.py:196
  1577.1 3.9 multiply_reduce_fusion.7
  1593.8 3.3 fusion.163
  1597.2 3.9 multiply_reduce_fusion.7
  1617.3 3.9 multiply_reduce_fusion.7
  1634.0 3.3 fusion.163
  1637.4 3.9 multiply_reduce_fusion.7
  1657.5 3.9 multiply_reduce_fusion.7
  1674.2 3.3 fusion.163
  1677.5 3.9 multiply_reduce_fusion.7
  1697.6 3.9 multiply_reduce_fusion.7
  1714.3 3.3 fusion.163
  1717.7 3.9 multiply_reduce_fusion.7
  1730.0 4.2 fusion.106
  1736.5 10.8 copy.74
  1747.3 8.2 reshape.198
  1755.5 7.3 copy.76
  1762.8 7.9 reshape.200
  1770.7 7.3 copy.75
  1778.1 7.9 reshape.199
  1789.1 8.8 convolution_convert_fusion.4
  1802.6 13.0 fusion.97
  1815.7 15.7 reduce-scatter.17.cloned.1.call-done
  1831.4 14.5 bitcast_convert_fusion
  1847.0 41.2 %all-reduce = (f32[2,1024]{1,0:T(2,128)S(1)}, f32[1024]{0:T(1024)}, f32[1024]{0:T(1024)}, f32[1024]{0:T(1024)}, f32[4096]{0:T(1024)S(1)}, /*index=5*/f32[1024]{0:T(1024)}, f32[1024]{0:T(1024)}, f32[1024]{0:T(1024)}) all-reduce(f32[2,1024]{1,0:T(2,128)S(1)} %maximum_dynamic-update-sl, ...), channel_id=1, replica_groups=mesh['replica'=2,'shard'=2,'tensor'=8] {'replica','shard','tensor'}, use_global_device_ids=true, to_apply=%region_23.24 | all-reduce | flops 12288 | bytes 98304 | tf_op jit(solution)/shard_map/psum | solution.py:256
  1897.5 156.9 %reduce-scatter.15.cloned.1.call-done = bf16[1024,1024]{1,0:T(8,128)(2,1)} async-done(((bf16[8192,1024]{1,0:T(8,128)(2,1)}), bf16[1024,1024]{1,0:T(8,128)(2,1)}) %reduce-scatter.15.cloned.1.call-update) | async-done | bytes 2097168 | tf_op jit(solution)/shard_map/reduce_scatter | solution.py:214
  2054.4 5.9 convert_add_fusion
  (245 shorter events, 222.5 us)
Async XLA Ops:
  8.0 156.2 %all-gather.7.cloned.1.call-start = ((), (), s32[]{:S(2)}) async-start(), calls=%async_computation.8 | async-start | bytes 18874368 | tf_op jit(solution)/shard_map/all_gather | solution.py:25
  8.7 462.5 %reduce-scatter.9.cloned.1.call-start = ((), (), s32[]{:S(2)}) async-start(), calls=%async_computation.9 | async-start | bytes 18874368 | tf_op jit(solution)/shard_map/reduce_scatter | solution.py:135
  18.3 278.0 %copy-start.12 = (bf16[128,1024]{1,0:T(8,128)(2,1)}, bf16[128,1024]{1,0:T(8,128)(2,1)S(1)}, u32[]{:S(2)}) copy-start(bf16[128,1024]{1,0:T(8,128)(2,1)S(1)} %all_gather.30) | copy-start | bytes 786436
  29.2 148.2 %copy-start.14 = (bf16[3,1024,128]{1,2,0:T(8,128)(2,1)}, bf16[3,1024,128]{1,2,0:T(8,128)(2,1)S(1)}, u32[]{:S(2)}) copy-start(bf16[3,1024,128]{1,2,0:T(8,128)(2,1)S(1)} %all_gather.28) | copy-start | bytes 2359300
  291.4 3.5 copy-start.7
  296.3 8.3 copy-start.5
  304.6 166.6 %copy-start = (bf16[1024,1024]{1,0:T(8,128)(2,1)S(1)}, bf16[1024,1024]{1,0:T(8,128)(2,1)}, u32[]{:S(2)}) copy-start(bf16[1024,1024]{1,0:T(8,128)(2,1)} %param.19) | copy-start | bytes 6291460
  304.7 166.6 %copy-start.16 = (f32[1024]{0:T(1024)S(1)}, f32[1024]{0:T(1024)}, u32[]{:S(2)}) copy-start(f32[1024]{0:T(1024)} %param.24) | copy-start | bytes 12292
  304.7 173.3 %all-gather.11.cloned.1.call-start = ((), (), s32[]{:S(2)}) async-start(), calls=%async_computation.11 | async-start | bytes 1572864 | tf_op jit(solution)/shard_map/all_gather | solution.py:19
  305.3 169.5 %copy-start.17 = (f32[1024]{0:T(1024)S(1)}, f32[1024]{0:T(1024)}, u32[]{:S(2)}) copy-start(f32[1024]{0:T(1024)} %param.25) | copy-start | bytes 12292
  305.3 169.5 %copy-start.21 = (f32[1024]{0:T(1024)S(1)}, f32[1024]{0:T(1024)}, u32[]{:S(2)}) copy-start(f32[1024]{0:T(1024)} %param.26) | copy-start | bytes 12292
  305.3 321.6 %all-gather.9.cloned.1.call-start = ((), (), s32[]{:S(2)}) async-start(), calls=%async_computation.10 | async-start | bytes 18874368 | tf_op jit(solution)/shard_map/all_gather | solution.py:29
  471.2 2.5 copy-start.1
  474.8 152.0 %copy-start.31 = (f32[512]{0:T(512)S(1)}, f32[512]{0:T(512)}, u32[]{:S(2)}) copy-start(f32[512]{0:T(512)} %param.28) | copy-start | bytes 6148
  477.3 196.9 %all-gather.13.cloned.1.call-start = ((), (), s32[]{:S(2)}) async-start(), calls=%async_computation.12 | async-start | bytes 1572864 | tf_op jit(solution)/shard_map/all_gather | solution.py:20
  477.9 377.5 %reduce-scatter.11.cloned.1.call-start = ((), (), s32[]{:S(2)}) async-start(), calls=%async_computation.13 | async-start | bytes 18874368 | tf_op jit(solution)/shard_map/reduce_scatter | solution.py:148
  689.0 166.4 %copy-start.27 = (f32[1024]{0:T(1024)S(1)}, f32[1024]{0:T(1024)}, u32[]{:S(2)}) copy-start(f32[1024]{0:T(1024)} %param.30) | copy-start | bytes 12292
  689.0 332.1 %all-gather.15.cloned.1.call-start = ((), (), s32[]{:S(2)}) async-start(), calls=%async_computation.14 | async-start | bytes 18874368 | tf_op jit(solution)/shard_map/all_gather | solution.py:161
  859.6 1.6 copy-start.8
  859.6 1.6 copy-start.20
  860.2 3.9 copy-start.26
  867.6 2.0 copy-start.4
  869.6 151.5 %copy-start.30 = (bf16[512,1024]{1,0:T(8,128)(2,1)S(1)}, bf16[512,1024]{1,0:T(8,128)(2,1)}, u32[]{:S(2)}) copy-start(bf16[512,1024]{1,0:T(8,128)(2,1)} %all-gather.13.cloned.1.call-done) | copy-start | bytes 3145732
  871.3 514.4 %reduce-scatter.13.cloned.1.call-start = ((), (), s32[]{:S(2)}) async-start(), calls=%async_computation.15 | async-start | bytes 37748736 | tf_op jit(solution)/shard_map/reduce_scatter | solution.py:178
  1021.1 22.3 %copy-start.29 = (bf16[1024,512]{1,0:T(8,128)(2,1)S(1)}, bf16[1024,512]{1,0:T(8,128)(2,1)}, u32[]{:S(2)}) copy-start(bf16[1024,512]{1,0:T(8,128)(2,1)} %all-gather.11.cloned.1.call-done) | copy-start | bytes 3145732
  1062.1 486.2 %all-gather.17.cloned.1.call-start = ((), (), s32[]{:S(2)}) async-start(), calls=%async_computation.16 | async-start | bytes 18874368 | tf_op jit(solution)/shard_map/all_gather | solution.py:189
  1385.7 6.6 copy-start.2
  1394.9 2.0 copy-start.3
  1398.5 417.1 %reduce-scatter.21.cloned.1.call-start = ((), (), s32[]{:S(2)}) async-start(), calls=%async_computation.20 | async-start | bytes 1572864 | tf_op jit(solution)/shard_map/reduce_scatter | solution.py:230
  1414.6 133.7 %copy-start.13 = (bf16[128,1024]{1,0:T(8,128)(2,1)S(1)}, bf16[128,1024]{1,0:T(8,128)(2,1)}, u32[]{:S(2)}) copy-start(bf16[128,1024]{1,0:T(8,128)(2,1)} %copy-done.12) | copy-start | bytes 786436
  1414.6 401.0 %reduce-scatter.23.cloned.1.call-start = ((), (), s32[]{:S(2)}) async-start(), calls=%async_computation.21 | async-start | bytes 1572864 | tf_op jit(solution)/shard_map/reduce_scatter | solution.py:233
  1430.8 384.8 %reduce-scatter.19.cloned.1.call-start = ((), (), s32[]{:S(2)}) async-start(), calls=%async_computation.19 | async-start | bytes 393216 | tf_op jit(solution)/shard_map/reduce_scatter | solution.py:227
  1730.0 4.6 copy-start.10
  1762.8 7.9 copy-start.11
  1778.1 11.0 copy-start.6
  1797.9 3.2 copy-start.9
  1797.9 33.5 %reduce-scatter.17.cloned.1.call-start = ((), (), s32[]{:S(2)}) async-start(), calls=%async_computation.18 | async-start | bytes 1179648 | tf_op jit(solution)/shard_map/reduce_scatter | solution.py:224
  1802.6 28.9 %copy-start.15 = (bf16[3,1024,128]{1,2,0:T(8,128)(2,1)S(1)}, bf16[3,1024,128]{1,2,0:T(8,128)(2,1)}, u32[]{:S(2)}) copy-start(bf16[3,1024,128]{1,2,0:T(8,128)(2,1)} %copy-done.14) | copy-start | bytes 2359300
  1815.6 73.9 %all-reduce.4.cloned.1.call-start = ((), (), s32[]{:S(2)}) async-start(), calls=%async_computation.22 | async-start | bytes 3145728 | tf_op jit(solution)/shard_map/psum | solution.py:238
  1831.4 223.0 %reduce-scatter.15.cloned.1.call-start = ((), (), s32[]{:S(2)}) async-start(), calls=%async_computation.17 | async-start | bytes 18874368 | tf_op jit(solution)/shard_map/reduce_scatter | solution.py:214
  1845.9 0.7 copy-start.28
  1845.9 1.0 copy-start.18
  1845.9 1.0 copy-start.19
  1845.9 1.1 copy-start.22
  1846.0 1.1 copy-start.23
  1846.0 1.1 copy-start.24
  1846.0 1.1 copy-start.25
Sparse Core Ops, SparseCore 0:
  10.4 153.7 all-gather.6
  304.8 166.3 reduce-scatter.8
  871.4 149.5 all-gather.14
  1398.7 149.6 all-gather.16
  1831.5 52.2 all-reduce.3
  1886.0 168.3 reduce-scatter.14
Sparse Core Ops, SparseCore 1:
  306.7 19.3 all-gather.10
  477.4 149.4 all-gather.8
  628.3 19.3 all-gather.12
  689.1 166.2 reduce-scatter.10
  1062.2 323.5 reduce-scatter.12
  1414.7 18.5 reduce-scatter.20
  1435.9 20.3 reduce-scatter.22
  1798.0 9.8 reduce-scatter.18
  1815.6 15.7 reduce-scatter.16
where the time goes:
time: 2080 us; the launch traced here: 2070 us
  waiting for transfers between devices  1380 us (66%)
  matrix products  381 us (18%)
  local copies, waits for them, and re-layouts  121 us (6%)
  other arithmetic  108 us (5%)
  blocking collectives  59.6 us (3%)
    reduce_scatter x1, waiting for transfers between devices, body(): lax.psum_scatter(lax.dot_general(row_block, w_up, CONTRACT_COLS, preferre...  324 us
    reduce_scatter x1, waiting for transfers between devices, body(): lax.psum_scatter(jnp.dot(row_block, w_down, preferred_element_type=jnp.fl...  166 us
    reduce_scatter x1, waiting for transfers between devices, body(): lax.psum_scatter(jnp.dot(row_block, w_out, preferred_element_type=jnp.flo...  166 us
    reduce_scatter x1, waiting for transfers between devices, body(): lax.psum_scatter(jnp.einsum('jtc,jdc->td', row_block, w_qkv, preferred_el...  157 us
    all_gather x1, waiting for transfers between devices, body(): rows_branch = lax.all_gather(branch_grad, 'tensor', axis=0, tiled=True)  150 us
    all_gather x1, waiting for transfers between devices, middle_rows(): return lax.all_gather(hidden_low, 'tensor', axis=0, tiled=True)  149 us
    all_gather x1, waiting for transfers between devices, input_rows(): return lax.all_gather(layer_input, 'tensor', axis=0, tiled=True)  135 us
    all_gather x1, waiting for transfers between devices, body(): rows_attn = lax.all_gather(attn_grad, 'tensor', axis=0, tiled=True)  117 us
  transfers between devices with their start and end apart: 15, of which 9 were waited for; matrix products, arithmetic and copies ran while one was open for 18% of the time, Pallas kernels for 0%

commit v1 on v0

--- a/solution.py
+++ b/solution.py
@@ -186,7 +186,17 @@
     )
     out_bias_part = jnp.sum(resid_one_grad, axis=0)
     attn_grad = resid_one_grad.astype(jnp.bfloat16)
-    rows_attn = lax.all_gather(attn_grad, "tensor", axis=0, tiled=True)
+    spare = lax.axis_size("tensor")
+    tall = lax.axis_index("tensor")
+    outer, plain, w1 = (spare, tall, attn_grad.shape[0])
+    w_next, odd = (attn_grad, 1)
+    while odd < outer:
+        taken_in = lax.ppermute(
+            w_next, "tensor", perm=[(kk, (kk - odd) % outer) for kk in range(outer)]
+        )
+        w_next = jnp.concatenate([w_next, taken_in], axis=0)
+        odd = 2 * odd
+    rows_attn = jnp.roll(w_next, plain * w1, axis=0)
     out_grad_part = lax.dot_general(
         mixed_rows, rows_attn, CONTRACT_ROWS, preferred_element_type=jnp.float32
     )

time: 2080 us -> 2440 us (1.17)
  waiting for transfers between devices: 1380 us -> 1710 us
  local copies, waits for them, and re-layouts: 121 us -> 146 us
    ppermute x0 -> x3, waiting for transfers between devices: none -> 440 us  [body(): lax.ppermute(w_next, 'tensor', perm=[(kk, (kk - odd) % outer) for kk in r...]
    all_gather x1 -> x0, waiting for transfers between devices: 117 us -> none  [body(): rows_attn = lax.all_gather(attn_grad, 'tensor', axis=0, tiled=True)]
  transfers between devices with their start and end apart: 15 -> 17, of which waited for: 9 -> 11; matrix products, arithmetic and copies ran while one was open for 18% -> 17% of each run, Pallas kernels for 0% -> 0%
where the time goes in v1:
time: 2440 us; the launch traced here: 2430 us
  waiting for transfers between devices  1710 us (70%)
  matrix products  381 us (16%)
  local copies, waits for them, and re-layouts  146 us (6%)
  other arithmetic  116 us (5%)
  blocking collectives  59.6 us (2%)
    ppermute x3, waiting for transfers between devices, body(): lax.ppermute(w_next, 'tensor', perm=[(kk, (kk - odd) % outer) for kk in r...  440 us
    reduce_scatter x1, waiting for transfers between devices, body(): lax.psum_scatter(lax.dot_general(row_block, w_up, CONTRACT_COLS, preferre...  324 us
    reduce_scatter x1, waiting for transfers between devices, body(): lax.psum_scatter(jnp.dot(row_block, w_down, preferred_element_type=jnp.fl...  166 us
    reduce_scatter x1, waiting for transfers between devices, body(): lax.psum_scatter(jnp.dot(row_block, w_out, preferred_element_type=jnp.flo...  166 us
    reduce_scatter x1, waiting for transfers between devices, body(): lax.psum_scatter(jnp.einsum('jtc,jdc->td', row_block, w_qkv, preferred_el...  157 us
    all_gather x1, waiting for transfers between devices, body(): rows_branch = lax.all_gather(branch_grad, 'tensor', axis=0, tiled=True)  150 us
    all_gather x1, waiting for transfers between devices, middle_rows(): return lax.all_gather(hidden_low, 'tensor', axis=0, tiled=True)  149 us
    all_gather x1, waiting for transfers between devices, input_rows(): return lax.all_gather(layer_input, 'tensor', axis=0, tiled=True)  135 us
  transfers between devices with their start and end apart: 17, of which 11 were waited for; matrix products, arithmetic and copies ran while one was open for 17% of the time, Pallas kernels for 0%

profile of v1, /device:TPU:0, one launch (start us, length us, event | category | flops | bytes accessed | tf_op | source)
XLA Modules:
  0.0 2429.1 jit_solution(14978242822464065466)
XLA Ops:
  10.9 7.4 all_gather.27
  18.3 10.9 all_gather.25
  29.3 135.0 %all-gather.6.cloned.1.call-done = bf16[8192,1024]{1,0:T(8,128)(2,1)} async-done(((bf16[1024,1024]{1,0:T(8,128)(2,1)}), bf16[8192,1024]{1,0:T(8,128)(2,1)}) %all-gather.6.cloned.1.call-update) | async-done | bytes 16777232 | tf_op jit(solution)/shard_map/all_gather | solution.py:25
  164.3 13.5 fusion.77
  180.2 4.4 fusion.116
  184.6 3.6 copy.81
  188.1 3.6 copy.80
  194.3 6.7 fusion.90
  201.0 90.2 %while.26 = (s32[]{:T(128)}, bf16[8,1024,2,64]{1,3,2,0:T(8,128)(2,1)}, f32[8,2,1024,1]{2,1,3,0:T(2,128)}, bf16[8,1024,2,64]{1,3,2,0:T(8,128)(2,1)}, s32[8,1024]{...) while((s32[]{:T(128)}, ...), condition=%wide.region_3.4_spmd, body=%wide.region_0.3_spmd.sunk | while | flops 563214336 | bytes 30488676 | solution.py:130
  207.2 4.4 fusion.161
  218.5 4.4 fusion.161
  229.8 4.4 fusion.161
  241.1 4.4 fusion.161
  252.4 4.4 fusion.161
  263.6 4.4 fusion.161
  274.9 4.4 fusion.161
  286.2 4.4 fusion.161
  296.2 8.5 convolution_convert_fusion
  305.4 165.8 %reduce-scatter.9.cloned.1.call-done = bf16[1024,1024]{1,0:T(8,128)(2,1)} async-done(((bf16[8192,1024]{1,0:T(8,128)(2,1)}), bf16[1024,1024]{1,0:T(8,128)(2,1)}) %reduce-scatter.9.cloned.1.call-update) | async-done | bytes 2097168 | tf_op jit(solution)/shard_map/reduce_scatter | solution.py:135
  479.6 148.9 %all-gather.8.cloned.1.call-done = bf16[8192,1024]{1,0:T(8,128)(2,1)} async-done(((bf16[1024,1024]{1,0:T(8,128)(2,1)}), bf16[8192,1024]{1,0:T(8,128)(2,1)}) %all-gather.8.cloned.1.call-update) | async-done | bytes 16777232 | tf_op jit(solution)/shard_map/all_gather | solution.py:29
  628.4 47.3 %fusion.56 = (bf16[8192,512]{1,0:T(8,128)(2,1)}, f32[8192,512]{1,0:T(8,128)}) fusion(f32[512]{0:T(512)S(1)} %copy-done.32, bf16[8192,1024]{1,0:T(8,128)(2,1)} %all-gather.8.cloned.1.call-done, bf16[1024,512]{1,0:T(8,128)(2,1)} %all-gather.10.cloned.1.call-done), kind=kOutput, calls=%fused_computation.68 | convolution fusion | flops 8866758656 | bytes 42993664 | tf_op jit(solution)/shard_map/dot_general | solution.py:145
  675.8 14.8 convolution_convert_fusion.1
  690.6 166.3 %reduce-scatter.11.cloned.1.call-done = bf16[1024,1024]{1,0:T(8,128)(2,1)} async-done(((bf16[8192,1024]{1,0:T(8,128)(2,1)}), bf16[1024,1024]{1,0:T(8,128)(2,1)}) %reduce-scatter.11.cloned.1.call-update) | async-done | bytes 2097168 | tf_op jit(solution)/shard_map/reduce_scatter | solution.py:148
  856.9 4.1 fusion.115
  864.5 3.6 fusion.112
  871.9 149.7 %all-gather.14.cloned.1.call-done = bf16[8192,1024]{1,0:T(8,128)(2,1)} async-done(((bf16[1024,1024]{1,0:T(8,128)(2,1)}), bf16[8192,1024]{1,0:T(8,128)(2,1)}) %all-gather.14.cloned.1.call-update) | async-done | bytes 16777232 | tf_op jit(solution)/shard_map/all_gather | solution.py:161
  1021.6 22.3 fusion.119
  1043.9 18.7 fusion.94
  1062.7 323.6 %reduce-scatter.13.cloned.1.call-done = f32[1024,1024]{1,0:T(8,128)} async-done(((f32[8192,1024]{1,0:T(8,128)}), f32[1024,1024]{1,0:T(8,128)}) %reduce-scatter.13.cloned.1.call-update) | async-done | bytes 4194320 | tf_op jit(solution)/shard_map/reduce_scatter | solution.py:178
  1386.3 6.7 multiply_reduce_fusion.1
  1399.7 23.6 collective-permute-done
  1425.5 91.1 %collective-permute-done.1 = bf16[2048,1024]{1,0:T(8,128)(2,1)S(1)} collective-permute-done((bf16[2048,1024]{1,0:T(8,128)(2,1)S(1)}, bf16[2048,1024]{1,0:T(8,128)(2,1)S(1)}, u32[]{:S(2)}, u32[]{:S(2)}) %collective-permute-start.1) | collective-permute-done | bytes 4194336 | tf_op jit(solution)/shard_map/ppermute | solution.py:194
  1516.5 4.5 pad_maximum_fusion
  1522.2 15.6 fusion.98
  1537.9 15.7 convolution_convert_fusion.2
  1559.4 325.0 %collective-permute-done.2 = bf16[4096,1024]{1,0:T(8,128)(2,1)} collective-permute-done((bf16[4096,1024]{1,0:T(8,128)(2,1)}, bf16[4096,1024]{1,0:T(8,128)(2,1)}, u32[]{:S(2)}, u32[]{:S(2)}) %collective-permute-start.2) | collective-permute-done | bytes 8388640 | tf_op jit(solution)/shard_map/ppermute | solution.py:194
  1884.4 7.6 constant_dynamic-update-slice_fusion.4
  1899.0 7.6 constant_dynamic-update-slice_fusion
  1906.6 8.3 fusion.80
  1918.3 9.1 copy.56
  1927.4 160.8 %while.27 = (s32[]{:T(128)}, f32[8,1024,2,64]{1,3,2,0:T(8,128)}, bf16[8,1024,2,64]{1,3,2,0:T(8,128)(2,1)}, f32[8,1024,2,64]{1,3,2,0:T(8,128)}, bf16[8,1024,2,64]...) while((s32[]{:T(128)}, f32[8,1024,2,64]{1,3,2,0:T(8,128)}, ...), condition=%wide.region_17.18_spmd, body=%wide.region_15.17_spmd.sunk | while | flops 1374943232 | bytes 70591616 | solution.py:206
  1935.3 3.9 multiply_reduce_fusion.7
  1955.4 3.9 multiply_reduce_fusion.7
  1975.5 3.9 multiply_reduce_fusion.7
  1995.5 3.9 multiply_reduce_fusion.7
  2015.6 3.9 multiply_reduce_fusion.7
  2035.7 3.9 multiply_reduce_fusion.7
  2055.8 3.9 multiply_reduce_fusion.7
  2075.8 3.9 multiply_reduce_fusion.7
  2088.1 4.0 fusion.117
  2092.1 7.3 copy.74
  2099.4 8.0 reshape.198
  2107.4 4.0 fusion.118
  2111.4 7.3 copy.76
  2118.7 7.8 reshape.200
  2126.5 10.9 copy.75
  2137.4 7.8 reshape.199
  2145.2 8.8 fusion.107
  2161.8 13.0 fusion.104
  2174.9 17.5 reduce-scatter.17.cloned.1.call-done
  2192.5 14.6 bitcast_convert_fusion
  2208.2 41.3 %all-reduce = (f32[2,1024]{1,0:T(2,128)S(1)}, f32[1024]{0:T(1024)}, f32[1024]{0:T(1024)}, f32[1024]{0:T(1024)}, f32[4096]{0:T(1024)S(1)}, /*index=5*/f32[1024]{0:T(1024)}, f32[1024]{0:T(1024)}, f32[1024]{0:T(1024)}) all-reduce(f32[2,1024]{1,0:T(2,128)S(1)} %maximum_dynamic-update-sl, ...), channel_id=1, replica_groups=mesh['replica'=2,'shard'=2,'tensor'=8] {'replica','shard','tensor'}, use_global_device_ids=true, to_apply=%region_23.24 | all-reduce | flops 12288 | bytes 98304 | tf_op jit(solution)/shard_map/psum | solution.py:266
  2258.7 156.8 %reduce-scatter.15.cloned.1.call-done = bf16[1024,1024]{1,0:T(8,128)(2,1)} async-done(((bf16[8192,1024]{1,0:T(8,128)(2,1)}), bf16[1024,1024]{1,0:T(8,128)(2,1)}) %reduce-scatter.15.cloned.1.call-update) | async-done | bytes 2097168 | tf_op jit(solution)/shard_map/reduce_scatter | solution.py:224
  2415.5 5.9 convert_add_fusion
  (259 shorter events, 257.4 us)
Async XLA Ops:
  8.0 156.2 %all-gather.6.cloned.1.call-start = ((), (), s32[]{:S(2)}) async-start(), calls=%async_computation.8 | async-start | bytes 18874368 | tf_op jit(solution)/shard_map/all_gather | solution.py:25
  8.7 462.5 %reduce-scatter.9.cloned.1.call-start = ((), (), s32[]{:S(2)}) async-start(), calls=%async_computation.9 | async-start | bytes 18874368 | tf_op jit(solution)/shard_map/reduce_scatter | solution.py:135
  18.3 277.8 %copy-start.13 = (bf16[128,1024]{1,0:T(8,128)(2,1)}, bf16[128,1024]{1,0:T(8,128)(2,1)S(1)}, u32[]{:S(2)}) copy-start(bf16[128,1024]{1,0:T(8,128)(2,1)S(1)} %all_gather.27) | copy-start | bytes 786436
  29.2 148.5 %copy-start.15 = (bf16[3,1024,128]{1,2,0:T(8,128)(2,1)}, bf16[3,1024,128]{1,2,0:T(8,128)(2,1)S(1)}, u32[]{:S(2)}) copy-start(bf16[3,1024,128]{1,2,0:T(8,128)(2,1)S(1)} %all_gather.25) | copy-start | bytes 2359300
  291.2 3.5 copy-start.10
  296.1 8.5 copy-start.8
  304.7 166.5 %copy-start = (bf16[1024,1024]{1,0:T(8,128)(2,1)S(1)}, bf16[1024,1024]{1,0:T(8,128)(2,1)}, u32[]{:S(2)}) copy-start(bf16[1024,1024]{1,0:T(8,128)(2,1)} %param.19) | copy-start | bytes 6291460
  304.7 166.5 %copy-start.17 = (f32[1024]{0:T(1024)S(1)}, f32[1024]{0:T(1024)}, u32[]{:S(2)}) copy-start(f32[1024]{0:T(1024)} %param.24) | copy-start | bytes 12292
  304.7 171.7 %copy-start.18 = (f32[1024]{0:T(1024)S(1)}, f32[1024]{0:T(1024)}, u32[]{:S(2)}) copy-start(f32[1024]{0:T(1024)} %param.25) | copy-start | bytes 12292
  304.7 171.7 %copy-start.22 = (f32[1024]{0:T(1024)S(1)}, f32[1024]{0:T(1024)}, u32[]{:S(2)}) copy-start(f32[1024]{0:T(1024)} %param.26) | copy-start | bytes 12292
  304.7 174.8 %all-gather.10.cloned.1.call-start = ((), (), s32[]{:S(2)}) async-start(), calls=%async_computation.11 | async-start | bytes 1572864 | tf_op jit(solution)/shard_map/all_gather | solution.py:19
  305.3 323.1 %all-gather.8.cloned.1.call-start = ((), (), s32[]{:S(2)}) async-start(), calls=%async_computation.10 | async-start | bytes 18874368 | tf_op jit(solution)/shard_map/all_gather | solution.py:29
  471.2 5.2 copy-start.1
  473.7 154.7 %copy-start.32 = (f32[512]{0:T(512)S(1)}, f32[512]{0:T(512)}, u32[]{:S(2)}) copy-start(f32[512]{0:T(512)} %param.28) | copy-start | bytes 6148
  478.9 196.9 %all-gather.12.cloned.1.call-start = ((), (), s32[]{:S(2)}) async-start(), calls=%async_computation.12 | async-start | bytes 1572864 | tf_op jit(solution)/shard_map/all_gather | solution.py:20
  479.5 377.4 %reduce-scatter.11.cloned.1.call-start = ((), (), s32[]{:S(2)}) async-start(), calls=%async_computation.13 | async-start | bytes 18874368 | tf_op jit(solution)/shard_map/reduce_scatter | solution.py:148
  690.6 166.3 %copy-start.28 = (f32[1024]{0:T(1024)S(1)}, f32[1024]{0:T(1024)}, u32[]{:S(2)}) copy-start(f32[1024]{0:T(1024)} %param.30) | copy-start | bytes 12292
  690.6 171.0 %copy-start.21 = (f32[1024]{0:T(1024)S(1)}, f32[1024]{0:T(1024)}, u32[]{:S(2)}) copy-start(f32[1024]{0:T(1024)} %param.31) | copy-start | bytes 12292
  690.6 331.0 %all-gather.14.cloned.1.call-start = ((), (), s32[]{:S(2)}) async-start(), calls=%async_computation.14 | async-start | bytes 18874368 | tf_op jit(solution)/shard_map/all_gather | solution.py:161
  856.9 4.7 copy-start.11
  861.0 3.5 copy-start.27
  868.1 2.0 copy-start.6
  868.1 153.5 %copy-start.31 = (bf16[512,1024]{1,0:T(8,128)(2,1)S(1)}, bf16[512,1024]{1,0:T(8,128)(2,1)}, u32[]{:S(2)}) copy-start(bf16[512,1024]{1,0:T(8,128)(2,1)} %all-gather.12.cloned.1.call-done) | copy-start | bytes 3145732
  871.8 514.5 %reduce-scatter.13.cloned.1.call-start = ((), (), s32[]{:S(2)}) async-start(), calls=%async_computation.15 | async-start | bytes 37748736 | tf_op jit(solution)/shard_map/reduce_scatter | solution.py:178
  1021.6 22.3 copy-start.30
  1062.6 1112.2 %reduce-scatter.21.cloned.1.call-start = ((), (), s32[]{:S(2)}) async-start(), calls=%async_computation.19 | async-start | bytes 1572864 | tf_op jit(solution)/shard_map/reduce_scatter | solution.py:240
  1386.3 6.7 copy-start.2
  1395.6 2.0 copy-start.3
  1399.6 122.6 %copy-start.7 = (bf16[1024,1024]{1,0:T(8,128)(2,1)}, bf16[1024,1024]{1,0:T(8,128)(2,1)S(1)}, u32[]{:S(2)}) copy-start(bf16[1024,1024]{1,0:T(8,128)(2,1)S(1)} %get-tuple-element.234) | copy-start | bytes 6291460
  1399.6 23.7 collective-permute-start
  1423.7 92.8 %collective-permute-start.1 = (bf16[2048,1024]{1,0:T(8,128)(2,1)S(1)}, bf16[2048,1024]{1,0:T(8,128)(2,1)S(1)}, u32[]{:S(2)}, u32[]{:S(2)}) collective-permute-start(bf16[2048,1024]{1,0:T(8,128)(2,1)S(1)} %pad_maximum_fusion.1), channel_id=1, source_target_pairs={{0,6},{1,7},{2,0},{3,1},{4,2},{5,3},{6,4},{7,5},{8,14},{9,15},{10,... | collective-permute-start | bytes 12582920 | tf_op jit(solution)/shard_map/ppermute | solution.py:194
  1516.5 4.5 copy-start.4
  1521.1 363.4 %collective-permute-start.2 = (bf16[4096,1024]{1,0:T(8,128)(2,1)}, bf16[4096,1024]{1,0:T(8,128)(2,1)}, u32[]{:S(2)}, u32[]{:S(2)}) collective-permute-start(bf16[4096,1024]{1,0:T(8,128)(2,1)} %pad_maximum_fusion), channel_id=1, source_target_pairs={{0,4},{1,5},{2,6},{3,7},{4,0},{5,1},{6,2},{7,3},{8,12},{9,13},{10,... | collective-permute-start | bytes 25165832 | tf_op jit(solution)/shard_map/ppermute | solution.py:194
  1537.8 637.0 %reduce-scatter.23.cloned.1.call-start = ((), (), s32[]{:S(2)}) async-start(), calls=%async_computation.20 | async-start | bytes 1572864 | tf_op jit(solution)/shard_map/reduce_scatter | solution.py:243
  1553.6 621.3 %reduce-scatter.19.cloned.1.call-start = ((), (), s32[]{:S(2)}) async-start(), calls=%async_computation.18 | async-start | bytes 393216 | tf_op jit(solution)/shard_map/reduce_scatter | solution.py:237
  1554.0 3.0 copy-start.5
  1899.0 7.6 copy-start.14
  2126.5 18.7 copy-start.9
  2154.0 6.3 copy-start.12
  2157.2 35.2 %reduce-scatter.17.cloned.1.call-start = ((), (), s32[]{:S(2)}) async-start(), calls=%async_computation.17 | async-start | bytes 1179648 | tf_op jit(solution)/shard_map/reduce_scatter | solution.py:234
  2161.7 30.8 %copy-start.16 = (bf16[3,1024,128]{1,2,0:T(8,128)(2,1)S(1)}, bf16[3,1024,128]{1,2,0:T(8,128)(2,1)}, u32[]{:S(2)}) copy-start(bf16[3,1024,128]{1,2,0:T(8,128)(2,1)} %copy-done.15) | copy-start | bytes 2359300
  2174.8 75.9 %all-reduce.4.cloned.1.call-start = ((), (), s32[]{:S(2)}) async-start(), calls=%async_computation.21 | async-start | bytes 3145728 | tf_op jit(solution)/shard_map/psum | solution.py:248
  2192.5 223.0 %reduce-scatter.15.cloned.1.call-start = ((), (), s32[]{:S(2)}) async-start(), calls=%async_computation.16 | async-start | bytes 18874368 | tf_op jit(solution)/shard_map/reduce_scatter | solution.py:224
  2207.1 0.7 copy-start.29
  2207.1 1.0 copy-start.19
  2207.1 1.0 copy-start.20
  2207.1 1.1 copy-start.23
  2207.1 1.1 copy-start.24
  2207.1 1.1 copy-start.25
  2207.2 1.1 copy-start.26
Sparse Core Ops, SparseCore 0:
  10.4 153.7 all-gather.5
  304.8 166.3 reduce-scatter.8
  871.9 149.5 all-gather.13
  2192.6 52.2 all-reduce.3
  2247.1 168.3 reduce-scatter.14
Sparse Core Ops, SparseCore 1:
  306.8 19.3 all-gather.9
  479.0 149.4 all-gather.7
  629.8 19.3 all-gather.11
  690.7 166.2 reduce-scatter.10
  1062.7 323.5 reduce-scatter.12
  1537.9 20.6 reduce-scatter.20
  1561.3 20.3 reduce-scatter.22
  2157.3 11.8 reduce-scatter.18
  2174.9 17.5 reduce-scatter.16
